TPU v7x, 512 devices: a whole 4x4x16 slice. The times are simulated.
512 devices in a mesh: lon: 32 (over z_lo, x), ch: 16 (over z_hi, y, core).
Axes of the slice: x: 4, y: 4, z: 16 (z_hi: 2, z_lo: 8; z = z_hi * 8 + z_lo), core: 2. Of those that a mesh axis runs over, the one named last changes fastest.
Arguments:
- inputs: bfloat16 [1, 4, 48, 64, 512], P(None, None, None, 'lon', 'ch'), may hold values from -6 to 6
- grad_out: bfloat16 [1, 4, 48, 64, 512], P(None, None, None, 'lon', 'ch'), may hold values from -6 to 6
- kernel: bfloat16 [3, 3, 3, 512, 512], P(None, None, None, 'ch'), may hold values from -0.0546875 to 0.0546875
Outputs:
- grad_in: bfloat16 [1, 4, 48, 64, 512], P(None, None, None, 'lon', 'ch')
- grad_kernel: float32 [3, 3, 3, 512, 512], P(None, None, None, 'ch', 'lon')
All inputs are finite; a program needn't handle non-finite values.
Results may differ from a plain program's by a relative error of at most 0.0012.
Values may be sent and summed in bfloat16 or wider, within the bound.
A program may use at most 64 MiB of HBM per device.

v0:
```python
import math

import jax
import jax.numpy as jnp
from jax import lax
from jax.sharding import PartitionSpec as P


def with_halo(cells, sides, width):
    for axis, dim in sides:
        count = lax.axis_size(axis)
        head = lax.slice_in_dim(cells, 0, width, axis=dim)
        tail = lax.slice_in_dim(cells, cells.shape[dim] - width, cells.shape[dim], axis=dim)
        cells = jnp.concatenate(
            [
                lax.ppermute(tail, axis, [(i, (i + 1) % count) for i in range(count)]),
                cells,
                lax.ppermute(head, axis, [((i + 1) % count, i) for i in range(count)]),
            ],
            axis=dim,
        )
    return cells


def contract_rows(left, right):
    return lax.dot_general(
        left, right, (((0,), (0,)), ((), ())), preferred_element_type=jnp.float32
    )


def tap_product(grad_all, kernel, step_t):
    out_width = grad_all.shape[4]
    cin_loc = kernel.shape[3]
    stacked = kernel[step_t].transpose(3, 0, 1, 2).reshape(out_width, 9 * cin_loc)
    product = jnp.dot(grad_all.reshape(-1, out_width), stacked, preferred_element_type=jnp.float32)
    return product.reshape(grad_all.shape[:4] + (3, 3, cin_loc))


def body(inputs, grad_out, kernel):
    batches, frames, lat_cells, lon_cols, cin_loc = inputs.shape
    lon_cells = lon_cols * lax.axis_size("lon")
    rscale = 1.0 / math.sqrt(batches * frames * lat_cells * lon_cells)
    grad_ext = with_halo(grad_out, (("lon", 3),), 1)
    grad_all = lax.all_gather(grad_ext, "ch", axis=4, tiled=True)
    out_width = grad_all.shape[4]
    accum_dx = jnp.zeros((batches, frames, lat_cells, lon_cols, cin_loc), jnp.float32)
    for step_t in range(3):
        product = tap_product(grad_all, kernel, step_t)
        padded = jnp.pad(product, ((0, 0), (1, 1), (1, 1), (0, 0), (0, 0), (0, 0), (0, 0)))
        for step_h in range(3):
            for step_w in range(3):
                accum_dx = (
                    accum_dx
                    + padded[
                        :,
                        2 - step_t : 2 - step_t + frames,
                        2 - step_h : 2 - step_h + lat_cells,
                        2 - step_w : 2 - step_w + lon_cols,
                        step_h,
                        step_w,
                        :,
                    ]
                )
    grad_in = accum_dx.astype(jnp.bfloat16)
    tap_terms = []
    shifted = jnp.stack(
        [
            jnp.pad(inputs, ((0, 0), (0, 0), (0, 0), (2 - step_w, step_w), (0, 0)))
            for step_w in range(3)
        ],
        axis=4,
    )
    x_pad = jnp.pad(shifted, ((0, 0), (1, 1), (1, 1), (0, 0), (0, 0), (0, 0)))
    flat_grad = grad_all.reshape(-1, out_width)
    for step_t in range(3):
        x_block = jnp.stack(
            [
                x_pad[:, step_t : step_t + frames, step_h : step_h + lat_cells]
                for step_h in range(3)
            ],
            axis=4,
        )
        tap_terms.append(
            contract_rows(x_block.reshape(-1, 9 * cin_loc), flat_grad).reshape(
                3, 3, cin_loc, out_width
            )
        )
    weight_terms = jnp.stack(tap_terms) * rscale
    grad_kernel = lax.psum_scatter(weight_terms, "lon", scatter_dimension=4, tiled=True)
    return (grad_in, grad_kernel)


def solution(mesh):
    return jax.shard_map(
        body,
        mesh=mesh,
        in_specs=(
            P(None, None, None, "lon", "ch"),
            P(None, None, None, "lon", "ch"),
            P(None, None, None, "ch", None),
        ),
        out_specs=(P(None, None, None, "lon", "ch"), P(None, None, None, "ch", "lon")),
        check_vma=False,
    )
```

profile of v0, /device:TPU:8, one launch (start us, length us, event | category | flops | bytes accessed | tf_op | source)
XLA Modules:
  0.0 632.7 jit_solution(9007344255820453416)
XLA Ops:
  9.5 15.3 %collective-permute-start.1 = (bf16[1,4,48,1,32]{2,3,1,0,4:T(2,128)(2,1)}, bf16[1,4,48,1,32]{2,3,1,0,4:T(2,128)(2,1)}, u32[]{:S(2)}, u32[]{:S(2)}) collective-permute-start(bf16[1,4,48,1,32]{2,3,1,0,4:T(2,128)(2,1)} %get-tuple-element.22), channel_id=1, source_target_pairs={{16,0},{32,16},{48,32},{64,48},{80,64},{96,80},{112,96},{128,112},... | collective-permute-start | bytes 36872 | tf_op jit(solution)/shard_map/ppermute | solution.py:18
  24.8 1.9 collective-permute-start
  26.7 1.0 pad_bitcast_fusion.2
  28.7 2.0 pad_maximum_fusion
  31.0 2.1 copy.59
  33.1 2.3 reshape.403
  35.4 2.0 copy.60
  37.4 2.1 copy.57
  39.5 2.3 reshape.401
  41.8 2.1 copy.58
  43.8 2.1 copy.54
  45.9 1.3 reshape.398
  47.2 1.0 copy.55
  48.2 1.1 pad_maximum_fusion.4
  49.4 49.3 %all_gather.3 = bf16[1,4,48,4,512]{2,3,1,0,4:T(4,128)(2,1)S(1)} all-gather(bf16[1,4,48,4,32]{2,3,1,0,4:T(4,128)(2,1)S(1)} %pad_maximum_fusion.4), channel_id=1, replica_groups=mesh['lon'=32,'ch'=16] {'ch'}, dimensions={4}, use_global_device_ids=true | all-gather | bytes 835584 | tf_op jit(solution)/shard_map/all_gather | solution.py:44
  98.7 2.9 copy.56
  101.5 1.6 reshape.421
  104.9 1.4 maximum_multiply_fusion
  106.3 8.7 %copy.61 = f32[3,3,3,32,512]{3,2,1,0,4:T(4,128)} copy(f32[3,3,3,32,512]{4,3,2,1,0:T(8,128)} %maximum_multiply_fusion) | data formatting | bytes 3538944 | tf_op jit(solution)/shard_map/mul | solution.py:88
  115.0 1.3 dynamic-slice
  116.9 1.8 copy.43
  118.8 1.8 convolution_bitcast_fusion
  122.2 1.2 fusion.61
  123.4 500.7 %all-reduce.10.cloned.1.call-done = f32[3,3,3,32,512]{3,2,1,0,4:T(4,128)} async-done(((f32[3,3,3,32,512]{3,2,1,0,4:T(4,128)}), f32[3,3,3,32,512]{3,2,1,0,4:T(4,128)}) %all-reduce.10.cloned.1.call-update) | async-done | bytes 1769488
  (32 shorter events, 8.5 us)
Async XLA Ops:
  7.2 617.0 %all-reduce.10.cloned.1.call-start = ((), (), s32[]{:S(2)}) async-start(), calls=%async_computation | async-start | bytes 18874368
  8.1 0.6 copy-start.5
  9.5 38.8 %collective-permute-start.1 = (bf16[1,4,48,1,32]{2,3,1,0,4:T(2,128)(2,1)}, bf16[1,4,48,1,32]{2,3,1,0,4:T(2,128)(2,1)}, u32[]{:S(2)}, u32[]{:S(2)}) collective-permute-start(bf16[1,4,48,1,32]{2,3,1,0,4:T(2,128)(2,1)} %get-tuple-element.22), channel_id=1, source_target_pairs={{16,0},{32,16},{48,32},{64,48},{80,64},{96,80},{112,96},{128,112},... | collective-permute-start | bytes 36872 | tf_op jit(solution)/shard_map/ppermute | solution.py:18
  24.8 23.4 %collective-permute-start = (bf16[1,4,48,1,32]{2,3,1,0,4:T(2,128)(2,1)}, bf16[1,4,48,1,32]{2,3,1,0,4:T(2,128)(2,1)}, u32[]{:S(2)}, u32[]{:S(2)}) collective-permute-start(bf16[1,4,48,1,32]{2,3,1,0,4:T(2,128)(2,1)} %get-tuple-element.21), channel_id=1, source_target_pairs={{0,16},{16,32},{32,48},{48,64},{64,80},{80,96},{96,112},{112,128},... | collective-permute-start | bytes 36872 | tf_op jit(solution)/shard_map/ppermute | solution.py:16
  33.1 4.3 copy-start.1
  39.5 4.4 copy-start
  45.9 2.3 copy-start.6
  98.7 4.4 copy-start.2
  103.1 1.0 copy-start.3
  103.1 1.4 copy-start.4
  118.8 1.8 copy-start.7
Sparse Core Ops, SparseCore 0:
  115.1 508.9 all-reduce.9
where the time goes:
time: 633 us
  waiting for transfers between devices  501 us (79%)
  blocking collectives  49.3 us (8%)
  local copies, waits for them, and re-layouts  39.7 us (6%)
  starting transfers between devices  17.3 us (3%)
  between operations  14.9 us (2%)
    unnamed x2, waiting for transfers between devices  501 us
    all_gather x1, blocking collectives, body(): grad_all = lax.all_gather(grad_ext, 'ch', axis=4, tiled=True)  49.3 us
    ppermute x1, starting transfers between devices, with_halo(): lax.ppermute(head, axis, [((i + 1) % count, i) for i in range(count)])  15.3 us
  transfers between devices with their start and end apart: 3, of which 1 were waited for; matrix products, arithmetic and copies ran while one was open for 5% of the time, Pallas kernels for 0%

commit v1 on v0

v1 whole, which is shorter than its diff:
```python
import functools
import math

import jax
import jax.numpy as jnp
from jax import lax
from jax.experimental import pallas as pl
from jax.experimental.pallas import tpu as pltpu
from jax.sharding import PartitionSpec as P

NX, NZ, NY, NH = 4, 8, 4, 2
MESH = pl.DeviceIdType.MESH
T, H, W, CI, CO = 4, 48, 2, 32, 16
COL = T * H
POS = W * COL


def shift_lanes(v, s):
    n = v.shape[1]
    s = s % n
    if s == 0:
        return v
    return jnp.concatenate([v[:, n - s:], v[:, :n - s]], axis=1)


def pack(ref):
    return jnp.concatenate([ref[t, w] for w in range(W) for t in range(T)], axis=1)


def kernel(rscale, x_ref, g_ref, k_ref, gin_ref, gk_ref,
           xg, gall, sx, gg, prod, zbuf, zl, zr, acc,
           swap_s, swap_r, gy_s, gy_r, core_s, core_r,
           xz_s, xz_r, xx_s, xx_r, ax_s, ax_r, az_s, az_r, ay_s, ay_r, ac_s, ac_r, ha_s, ha_r):
    lon, ch = lax.axis_index("lon"), lax.axis_index("ch")
    z, x = lon // NX, lon % NX
    zh, y, core = ch // (2 * NY), (ch // 2) % NY, ch % 2

    def at(z=z, x=x, zh=zh, y=y, core=core):
        return (z * NX + x, (zh * NY + y) * 2 + core)

    swap_id = at(zh=1 - zh)
    sib_id = at(core=1 - core)
    left_id = (lax.rem(lon + NX * NZ - 1, NX * NZ), ch)
    right_id = (lax.rem(lon + 1, NX * NZ), ch)
    y_ids = [at(y=lax.rem(y + d, NY)) for d in range(1, NY)]
    z_ids = [at(z=lax.rem(z + d, NZ)) for d in range(1, NZ)]
    x_ids = [at(x=lax.rem(x + d, NX)) for d in range(1, NX)]
    partners = [swap_id, sib_id, left_id, right_id] + y_ids + z_ids + x_ids

    barrier = pltpu.get_barrier_semaphore()
    for dev in partners:
        pl.semaphore_signal(barrier, inc=1, device_id=dev, device_id_type=MESH)

    def remote(src, dst, ss, rs, dev):
        return pltpu.make_async_remote_copy(
            src_ref=src, dst_ref=dst, send_sem=ss, recv_sem=rs, device_id=dev, device_id_type=MESH)

    gall[zh, y, core] = pack(g_ref)
    xg[x, z] = pack(x_ref)
    pl.semaphore_wait(barrier, len(partners))

    sends = []

    def go(copy):
        copy.start()
        sends.append(copy)
        return copy

    mine = gall.at[zh, y, core]
    swap = go(remote(mine, mine, swap_s, swap_r, swap_id))
    gy = [go(remote(mine, mine, gy_s.at[0, d], gy_r.at[0, d], y_ids[d])) for d in range(NY - 1)]
    own = xg.at[x, z]
    xz = [go(remote(own, own, xz_s.at[d], xz_r.at[d], z_ids[d])) for d in range(NZ - 1)]
    xx = []
    for d in range(NX - 1):
        xx.append(go(remote(own, own, xx_s.at[0, d], xx_r.at[0, d], x_ids[d])))
    swap.wait_recv()
    other = gall.at[1 - zh, y, core]
    gy += [go(remote(other, other, gy_s.at[1, d], gy_r.at[1, d], y_ids[d])) for d in range(NY - 1)]
    for c in gy:
        c.wait_recv()
    half = gall.at[:, :, core]
    sib = go(remote(half, half, core_s, core_r, sib_id))

    carries = core == x // 2

    def ax_copy(r, dev):
        return remote(gall.at[:, :, core, pl.ds(CO * r, CO)], sx, ax_s.at[r], ax_r, dev)

    @pl.when(x == y)
    def _():
        for r in range(2):
            xd = core * 2 + r

            @pl.when(xd != x)
            def _():
                ax_copy(r, at(x=xd)).start()

            @pl.when(xd == x)
            def _():
                sx[...] = gall[:, :, core, CO * r:CO * (r + 1)]

    for d in range(NZ - 1):
        xz[d].wait_recv()
        blk = xg.at[x, lax.rem(z + NZ - 1 - d, NZ)]
        for e in range(NX - 1):
            xx.append(go(remote(blk, blk, xx_s.at[d + 1, e], xx_r.at[d + 1, e], x_ids[e])))

    def az_copy(d):
        zd = lax.rem(z + d + 1, NZ)
        return remote(sx.at[zd // NY, lax.rem(zd, NY)], gg.at[y, z], az_s.at[d], az_r.at[d], z_ids[d])

    @pl.when(carries)
    def _():
        @pl.when(x != y)
        def _():
            ax_copy(0, sib_id).wait_recv()
        for d in range(NZ - 1):
            az_copy(d).start()
        gg[y, z] = sx[z // NY, lax.rem(z, NY)]

    sib.wait_recv()
    lane = lax.broadcasted_iota(jnp.int32, (1, POS), 1)
    hh = lax.rem(lane, H)
    tt = lax.rem(lane // H, T)
    low = lane < COL
    prod[...] = jnp.dot(k_ref[...], gall[...].reshape(NH * NY * 2 * CI, POS), preferred_element_type=jnp.float32)

    def tap(a, c, e):
        r = ((a * 3 + c) * 3 + e) * CI
        return prod[r:r + CI, :]

    sums = []
    for e in range(3):
        total = None
        for a in range(3):
            part = tap(a, 1, e)
            part += jnp.where(hh != H - 1, shift_lanes(tap(a, 0, e), -1), 0.0)
            part += jnp.where(hh != 0, shift_lanes(tap(a, 2, e), 1), 0.0)
            if a == 0:
                part = jnp.where(tt != T - 1, shift_lanes(part, -H), 0.0)
            elif a == 2:
                part = jnp.where(tt != 0, shift_lanes(part, H), 0.0)
            total = part if total is None else total + part
        sums.append(total)
    zbuf[...] = jnp.where(low, sums[0], sums[2])
    to_left = go(remote(zbuf, zr, ha_s.at[0], ha_r.at[0], left_id))
    to_right = go(remote(zbuf, zl, ha_s.at[1], ha_r.at[1], right_id))

    def ay_copy(d):
        slab = gg.at[y]
        return remote(slab, slab, ay_s.at[d], ay_r.at[d], y_ids[d])

    def ac_copy(d):
        slab = gg.at[lax.rem(y + NY - d, NY)]
        return remote(slab, slab, ac_s.at[d], ac_r.at[d], sib_id)

    @pl.when(carries)
    def _():
        for d in range(NZ - 1):
            az_copy(d).wait_recv()
        for d in range(NY - 1):
            ay_copy(d).start()
        ac_copy(0).start()
        for d in range(NY - 1):
            ay_copy(d).wait_recv()
            ac_copy(d + 1).start()

    @pl.when(jnp.logical_not(carries))
    def _():
        for d in range(NY):
            ac_copy(d).wait_recv()

    to_left.wait_recv()
    to_right.wait_recv()
    grad = sums[1] + shift_lanes(jnp.where(low, sums[2] + zr[...], sums[0] + zl[...]), COL)
    grad = grad.astype(jnp.bfloat16)
    for w in range(W):
        for t in range(T):
            o = w * COL + t * H
            gin_ref[t, w] = grad[:, o:o + H]

    for c in xx:
        c.wait_recv()

    zero = jnp.zeros((), jnp.bfloat16)
    acc[...] = jnp.zeros_like(acc)

    @pl.loop(0, NZ)
    def _(zz):
        for xs in range(NX):
            xb = xg[xs, zz]
            x0 = jnp.where(hh != 0, shift_lanes(xb, 1), zero)
            x2 = jnp.where(hh != H - 1, shift_lanes(xb, -1), zero)
            rows = jnp.concatenate([x0, xb, x2], axis=0)
            here = gg[xs, zz]
            after = gg[xs + 1, zz] if xs < NX - 1 else gg[0, lax.rem(zz + 1, NZ)]
            before = gg[xs - 1, zz] if xs > 0 else gg[NX - 1, lax.rem(zz + NZ - 1, NZ)]
            rh = shift_lanes(here, COL)
            e0 = jnp.where(low, rh, shift_lanes(after, COL))
            e2 = jnp.where(low, shift_lanes(before, COL), rh)
            ge = jnp.concatenate([e0, here, e2], axis=0)
            a0 = jnp.where(tt != T - 1, shift_lanes(ge, -H), zero)
            a2 = jnp.where(tt != 0, shift_lanes(ge, H), zero)
            gs = jnp.concatenate([a0, ge, a2], axis=0)
            acc[...] += lax.dot_general(gs, rows, (((1,), (1,)), ((), ())), preferred_element_type=jnp.float32)

    for a in range(3):
        for e in range(3):
            r = (a * 3 + e) * CO
            for c in range(3):
                gk_ref[(a * 3 + c) * 3 + e] = acc[r:r + CO, c * CI:(c + 1) * CI] * rscale

    for c in sends:
        c.wait_send()

    @pl.when(x == y)
    def _():
        for r in range(2):
            @pl.when(core * 2 + r != x)
            def _():
                ax_copy(r, sib_id).wait_send()

    @pl.when(carries)
    def _():
        for d in range(NZ - 1):
            az_copy(d).wait_send()
        for d in range(NY - 1):
            ay_copy(d).wait_send()
        for d in range(NY):
            ac_copy(d).wait_send()


def body(inputs, grad_out, weights):
    rscale = 1.0 / math.sqrt(T * H * W * NX * NZ)
    xs = inputs.transpose(0, 1, 3, 4, 2).reshape(T, W, CI, H)
    gs = grad_out.transpose(0, 1, 3, 4, 2).reshape(T, W, CI, H)
    ks = weights.reshape(27 * CI, 512)
    dma = pltpu.SemaphoreType.DMA
    gin, gk = pl.pallas_call(
        functools.partial(kernel, rscale),
        out_shape=(jax.ShapeDtypeStruct((T, W, CI, H), jnp.bfloat16),
                   jax.ShapeDtypeStruct((27, CO, CI), jnp.float32)),
        in_specs=[pl.BlockSpec(memory_space=pltpu.VMEM)] * 3,
        out_specs=(pl.BlockSpec(memory_space=pltpu.VMEM),) * 2,
        scratch_shapes=[
            pltpu.VMEM((NX, NZ, CI, POS), jnp.bfloat16),
            pltpu.VMEM((NH, NY, 2, CI, POS), jnp.bfloat16),
            pltpu.VMEM((NH, NY, CO, POS), jnp.bfloat16),
            pltpu.VMEM((NX, NZ, CO, POS), jnp.bfloat16),
            pltpu.VMEM((27 * CI, POS), jnp.float32),
            pltpu.VMEM((CI, POS), jnp.float32),
            pltpu.VMEM((CI, POS), jnp.float32),
            pltpu.VMEM((CI, POS), jnp.float32),
            pltpu.VMEM((9 * CO, 3 * CI), jnp.float32),
            dma, dma, dma((2, NY - 1)), dma((2, NY - 1)), dma, dma,
            dma((NZ - 1,)), dma((NZ - 1,)), dma((NZ, NX - 1)), dma((NZ, NX - 1)),
            dma((2,)), dma, dma((NZ - 1,)), dma((NZ - 1,)),
            dma((NY - 1,)), dma((NY - 1,)), dma((NY,)), dma((NY,)), dma((2,)), dma((2,)),
        ],
        compiler_params=pltpu.CompilerParams(
            collective_id=0, has_side_effects=True, vmem_limit_bytes=32 << 20),
    )(xs, gs, ks)
    grad_in = gin.reshape(1, T, W, CI, H).transpose(0, 1, 4, 2, 3)
    grad_kernel = gk.reshape(3, 3, 3, CO, CI).transpose(0, 1, 2, 4, 3)
    return grad_in, grad_kernel


def solution(mesh):
    return jax.shard_map(
        body,
        mesh=mesh,
        in_specs=(
            P(None, None, None, "lon", "ch"),
            P(None, None, None, "lon", "ch"),
            P(None, None, None, "ch", None),
        ),
        out_specs=(P(None, None, None, "lon", "ch"), P(None, None, None, "ch", "lon")),
        check_vma=False,
    )
```

time: 633 us -> 60.2 us (0.10)
  the two profiles are of different devices: /device:TPU:8 before, /device:TPU:1 now
where the time goes in v1:
time: 60.2 us; the launch traced here: 59.9 us
  Pallas kernels  55.1 us (92%)
  local copies, waits for them, and re-layouts  4.16 us (7%)
  between operations  0.65 us (1%)
    pallas_call x1, Pallas kernels, body(): pl.pallas_call(functools.partial(kernel, rscale), out_shape=(jax.ShapeDty...  55.1 us
    unnamed x8, local copies, waits for them, and re-layouts  4.16 us

profile of v1, /device:TPU:1, one launch (start us, length us, event | category | flops | bytes accessed | tf_op | source)
XLA Modules:
  0.0 59.9 jit_solution(13935710191957698614)
XLA Ops:
  0.6 0.0 copy-start
  0.6 1.2 %copy-done = bf16[3,3,3,32,512]{4,3,2,1,0:T(8,128)(2,1)S(1)} copy-done((bf16[3,3,3,32,512]{4,3,2,1,0:T(8,128)(2,1)S(1)}, bf16[3,3,3,32,512]{4,3,2,1,0:T(8,128)(2,1)}, u32[]{:S(2)}) %copy-start) | copy-done | bytes 884760
  1.8 0.0 copy-start.1
  1.8 0.8 %copy-done.1 = bf16[1,4,48,2,32]{2,4,3,1,0:T(8,128)(2,1)S(1)} copy-done((bf16[1,4,48,2,32]{2,4,3,1,0:T(8,128)(2,1)S(1)}, bf16[1,4,48,2,32]{2,4,3,1,0:T(8,128)(2,1)}, u32[]{:S(2)}) %copy-start.1) | copy-done | bytes 24600
  2.6 0.0 copy-start.2
  2.6 0.8 %copy-done.2 = bf16[1,4,48,2,32]{2,4,3,1,0:T(8,128)(2,1)S(1)} copy-done((bf16[1,4,48,2,32]{2,4,3,1,0:T(8,128)(2,1)S(1)}, bf16[1,4,48,2,32]{2,4,3,1,0:T(8,128)(2,1)}, u32[]{:S(2)}) %copy-start.2) | copy-done | bytes 24600
  3.5 55.1 %shard_map.50 = (bf16[4,2,32,48]{3,2,1,0:T(8,128)(2,1)S(1)}, f32[27,16,32]{2,1,0:T(8,128)S(1)}) custom-call(bf16[4,2,32,48]{3,2,1,0:T(8,128)(2,1)S(1)} %bitcast.15, bf16[4,2,32,48]{3,2,1,0:T(8,128)(2,1)S(1)} %bitcast.16, bf16[864,512]{1,0:T(8,128)(2,1)S(1)} %bitcast.13), custom_call_target="tpu_custom_call" | custom-call | tf_op jit(solution)/shard_map/pallas_call | solution.py:240
  58.6 0.6 %copy.7 = bf16[1,4,48,2,32]{2,4,3,1,0:T(8,128)(2,1)} copy(bf16[1,4,48,2,32]{2,4,3,1,0:T(8,128)(2,1)S(1)} %bitcast.17) | data formatting | bytes 49152
  59.3 0.7 %copy.8 = f32[3,3,3,32,16]{3,4,2,1,0:T(8,128)} copy(f32[3,3,3,32,16]{3,4,2,1,0:T(8,128)S(1)} %bitcast.14) | data formatting | bytes 110592
Async XLA Ops:
  0.6 1.2 %copy-start = (bf16[3,3,3,32,512]{4,3,2,1,0:T(8,128)(2,1)S(1)}, bf16[3,3,3,32,512]{4,3,2,1,0:T(8,128)(2,1)}, u32[]{:S(2)}) copy-start(bf16[3,3,3,32,512]{4,3,2,1,0:T(8,128)(2,1)} %param.5) | copy-start | bytes 2654212
  1.8 0.8 %copy-start.1 = (bf16[1,4,48,2,32]{2,4,3,1,0:T(8,128)(2,1)S(1)}, bf16[1,4,48,2,32]{2,4,3,1,0:T(8,128)(2,1)}, u32[]{:S(2)}) copy-start(bf16[1,4,48,2,32]{2,4,3,1,0:T(8,128)(2,1)} %param.3) | copy-start | bytes 73732
  2.6 0.8 %copy-start.2 = (bf16[1,4,48,2,32]{2,4,3,1,0:T(8,128)(2,1)S(1)}, bf16[1,4,48,2,32]{2,4,3,1,0:T(8,128)(2,1)}, u32[]{:S(2)}) copy-start(bf16[1,4,48,2,32]{2,4,3,1,0:T(8,128)(2,1)} %param.4) | copy-start | bytes 73732

commit v2 on v1

v2 whole, which is shorter than its diff:
```python
import functools
import math

import jax
import jax.numpy as jnp
from jax import lax
from jax.experimental import pallas as pl
from jax.experimental.pallas import tpu as pltpu
from jax.sharding import PartitionSpec as P

NX, NZ, NY, NH = 4, 8, 4, 2
MESH = pl.DeviceIdType.MESH
T, H, W, CI, CO = 4, 48, 2, 32, 16
COL = T * H
POS = W * COL
HALF = NY * 2 * CI
NEAR = (0, 6, 1, 5, 2, 4, 3)


def shift_lanes(v, s):
    n = v.shape[1]
    s = s % n
    if s == 0:
        return v
    return jnp.concatenate([v[:, n - s:], v[:, :n - s]], axis=1)


def pack(ref):
    return jnp.concatenate([ref[t, w] for w in range(W) for t in range(T)], axis=1)


def kernel(rscale, x_hbm, g_hbm, k_hbm, gin_ref, gk_ref,
           x_ref, g_ref, k_ref, xg, xs, gall, abuf, gg, prod, zbuf, zl, zr, acc,
           load_s, swap_s, swap_r, gy_s, gy_r, core_s, core_r,
           xz_s, xz_r, xx_s, xx_r, a_s, a_r, b_s, b_r, ay_s, ay_r, ac_s, ac_r, ha_s, ha_r):
    lon, ch = lax.axis_index("lon"), lax.axis_index("ch")
    z, x = lon // NX, lax.rem(lon, NX)
    zh, y, core = ch // (2 * NY), lax.rem(ch // 2, NY), lax.rem(ch, 2)

    def at(z=z, x=x, zh=zh, y=y, core=core):
        return (z * NX + x, (zh * NY + y) * 2 + core)

    swap_id = at(zh=1 - zh)
    sib_id = at(core=1 - core)
    left_id = (lax.rem(lon + NX * NZ - 1, NX * NZ), ch)
    right_id = (lax.rem(lon + 1, NX * NZ), ch)
    y_ids = [at(y=lax.rem(y + d, NY)) for d in range(1, NY)]
    z_ids = [at(z=lax.rem(z + d, NZ)) for d in range(1, NZ)]
    x_ids = [at(x=lax.rem(x + d, NX)) for d in range(1, NX)]
    partners = [swap_id, sib_id, left_id, right_id] + y_ids + z_ids + x_ids

    turn = y == lax.rem(z, NY)
    home = zh == z // NY
    carries = core == x // 2
    b_from = at(x=y, y=lax.rem(z, NY))
    b_self = turn & (x == y)

    barrier = pltpu.get_barrier_semaphore()

    def greet(dev):
        pl.semaphore_signal(barrier, inc=1, device_id=dev, device_id_type=MESH)

    for dev in partners:
        greet(dev)

    @pl.when(turn & jnp.logical_not(home))
    def _():
        for s in range(NZ):
            greet(at(z=s, zh=1 - zh))

    @pl.when(carries & jnp.logical_not(b_self))
    def _():
        greet(b_from)

    load_g = pltpu.make_async_copy(g_hbm, g_ref, load_s.at[0])
    load_x = pltpu.make_async_copy(x_hbm, x_ref, load_s.at[1])
    load_k = pltpu.make_async_copy(k_hbm, k_ref, load_s.at[2])
    load_g.start()
    load_x.start()
    load_k.start()

    def remote(src, dst, ss, rs, dev):
        return pltpu.make_async_remote_copy(
            src_ref=src, dst_ref=dst, send_sem=ss, recv_sem=rs, device_id=dev, device_id_type=MESH)

    load_g.wait()
    gall[zh, y, core] = pack(g_ref)
    load_x.wait()
    xg[x, z] = pack(x_ref)
    pl.semaphore_wait(barrier, len(partners) + 1 + jnp.where(turn, 2 - (carries & (x == y)).astype(jnp.int32), 0))

    sends = []

    def go(copy):
        copy.start()
        sends.append(copy)
        return copy

    mine = gall.at[zh, y, core]
    swap = go(remote(mine, mine, swap_s, swap_r, swap_id))
    a_z = zh * NY + y
    go(remote(mine, abuf.at[z], a_s.at[0], a_r.at[z], at(z=a_z, zh=1 - zh)))

    def a_near():
        return remote(mine, abuf.at[z], a_s.at[1], a_r.at[z], at(z=a_z))

    @pl.when(a_z != z)
    def _():
        a_near().start()

    @pl.when(a_z == z)
    def _():
        abuf[z] = gall[zh, y, core]

    gy = [go(remote(mine, mine, gy_s.at[0, d], gy_r.at[0, d], y_ids[d])) for d in range(NY - 1)]
    own = xg.at[x, z]
    xz = {d: go(remote(own, own, xz_s.at[d], xz_r.at[d], z_ids[d])) for d in NEAR}
    xx = [go(remote(own, own, xx_s.at[0, e], xx_r.at[0, e], x_ids[e])) for e in range(NX - 1)]

    def pass_x(ds):
        for d in ds:
            xz[d].wait_recv()
            blk = xg.at[x, lax.rem(z + NZ - 1 - d, NZ)]
            for e in range(NX - 1):
                xx.append(go(remote(blk, blk, xx_s.at[d + 1, e], xx_r.at[d + 1, e], x_ids[e])))

    def to_core(h, i):
        part = gall.at[h, :, core]
        return go(remote(part, part, core_s.at[i], core_r.at[i], sib_id))

    for c in gy:
        c.wait_recv()
    sib0 = to_core(zh, 0)
    pass_x(NEAR[:4])

    swap.wait_recv()
    other = gall.at[1 - zh, y, core]
    gy1 = [go(remote(other, other, gy_s.at[1, d], gy_r.at[1, d], y_ids[d])) for d in range(NY - 1)]

    def b_copy(r):
        return remote(abuf.at[:, pl.ds(CO * r, CO)], gg.at[x], b_s.at[r], b_r, at(x=core * 2 + r, y=x))

    def b_here(r):
        return (core * 2 + r == x) & (x == y)

    @pl.when(turn)
    def _():
        for s in range(NZ):
            @pl.when(jnp.logical_not(home & (z == s)))
            def _():
                remote(mine, abuf.at[s], a_s.at[0], a_r.at[s], sib_id).wait_recv()
        for r in range(2):
            @pl.when(jnp.logical_not(b_here(r)))
            def _():
                b_copy(r).start()

            @pl.when(b_here(r))
            def _():
                gg[x] = abuf[:, CO * r:CO * (r + 1)]

    pass_x(NEAR[4:])

    lane = lax.broadcasted_iota(jnp.int32, (1, POS), 1)
    hh = lax.rem(lane, H)
    tt = lax.rem(lane // H, T)
    low = lane < COL

    def half_product(h):
        cols = pl.ds(pl.multiple_of(h * HALF, HALF), HALF)
        return jnp.dot(k_ref[:, cols], gall[h].reshape(HALF, POS), preferred_element_type=jnp.float32)

    load_k.wait()
    sib0.wait_recv()
    prod[...] = half_product(zh)
    for c in gy1:
        c.wait_recv()
    sib1 = to_core(1 - zh, 1)
    sib1.wait_recv()
    prod[...] += half_product(1 - zh)

    def tap(a, c, e):
        r = ((a * 3 + c) * 3 + e) * CI
        return prod[r:r + CI, :]

    def tap_sum(e):
        total = None
        for a in range(3):
            part = tap(a, 1, e)
            part += jnp.where(hh != H - 1, shift_lanes(tap(a, 0, e), -1), 0.0)
            part += jnp.where(hh != 0, shift_lanes(tap(a, 2, e), 1), 0.0)
            if a == 0:
                part = jnp.where(tt != T - 1, shift_lanes(part, -H), 0.0)
            elif a == 2:
                part = jnp.where(tt != 0, shift_lanes(part, H), 0.0)
            total = part if total is None else total + part
        return total

    sum0, sum2 = tap_sum(0), tap_sum(2)
    zbuf[...] = jnp.where(low, sum0, sum2)
    to_left = go(remote(zbuf, zr, ha_s.at[0], ha_r.at[0], left_id))
    to_right = go(remote(zbuf, zl, ha_s.at[1], ha_r.at[1], right_id))

    def ay_copy(d):
        slab = gg.at[y]
        return remote(slab, slab, ay_s.at[d], ay_r.at[d], y_ids[d])

    def ac_copy(d):
        slab = gg.at[lax.rem(y + NY - d, NY)]
        return remote(slab, slab, ac_s.at[d], ac_r.at[d], sib_id)

    @pl.when(carries)
    def _():
        @pl.when(jnp.logical_not(b_self))
        def _():
            b_copy(0).wait_recv()
        for d in range(NY - 1):
            ay_copy(d).start()
        ac_copy(0).start()

    mid = tap_sum(1)
    inner = jnp.where(low, sum2, sum0)
    for c in xx:
        c.wait_recv()
    zero = jnp.zeros((), jnp.bfloat16)

    @pl.loop(0, NX * NZ)
    def _(i):
        xb = xg[i // NZ, lax.rem(i, NZ)]
        xs[i, 0:CI] = jnp.where(hh != 0, shift_lanes(xb, 1), zero)
        xs[i, CI:2 * CI] = xb
        xs[i, 2 * CI:] = jnp.where(hh != H - 1, shift_lanes(xb, -1), zero)

    @pl.when(carries)
    def _():
        for d in range(NY - 1):
            ay_copy(d).wait_recv()
            ac_copy(d + 1).start()

    to_left.wait_recv()
    to_right.wait_recv()
    grad = mid + shift_lanes(inner + jnp.where(low, zr[...], zl[...]), COL)
    grad = grad.astype(jnp.bfloat16)
    for w in range(W):
        for t in range(T):
            o = w * COL + t * H
            gin_ref[t, w] = grad[:, o:o + H]

    @pl.when(jnp.logical_not(carries))
    def _():
        for d in range(NY):
            ac_copy(d).wait_recv()

    acc[...] = jnp.zeros_like(acc)

    @pl.loop(0, NZ)
    def _(zz):
        for xn in range(NX):
            here = gg[xn, zz]
            after = gg[xn + 1, zz] if xn < NX - 1 else gg[0, lax.rem(zz + 1, NZ)]
            before = gg[xn - 1, zz] if xn > 0 else gg[NX - 1, lax.rem(zz + NZ - 1, NZ)]
            rh = shift_lanes(here, COL)
            e0 = jnp.where(low, rh, shift_lanes(after, COL))
            e2 = jnp.where(low, shift_lanes(before, COL), rh)
            ge = jnp.concatenate([e0, here, e2], axis=0)
            a0 = jnp.where(tt != T - 1, shift_lanes(ge, -H), zero)
            a2 = jnp.where(tt != 0, shift_lanes(ge, H), zero)
            gs = jnp.concatenate([a0, ge, a2], axis=0)
            acc[...] += lax.dot_general(
                gs, xs[xn * NZ + zz], (((1,), (1,)), ((), ())), preferred_element_type=jnp.float32)

    for a in range(3):
        for e in range(3):
            r = (a * 3 + e) * CO
            for c in range(3):
                gk_ref[(a * 3 + c) * 3 + e] = acc[r:r + CO, c * CI:(c + 1) * CI] * rscale

    for c in sends:
        c.wait_send()

    @pl.when(a_z != z)
    def _():
        a_near().wait_send()

    @pl.when(turn)
    def _():
        for r in range(2):
            @pl.when(jnp.logical_not(b_here(r)))
            def _():
                b_copy(r).wait_send()

    @pl.when(carries)
    def _():
        for d in range(NY - 1):
            ay_copy(d).wait_send()
        for d in range(NY):
            ac_copy(d).wait_send()


def body(inputs, grad_out, weights):
    rscale = 1.0 / math.sqrt(T * H * W * NX * NZ)
    xt = inputs.transpose(0, 1, 3, 4, 2).reshape(T, W, CI, H)
    gt = grad_out.transpose(0, 1, 3, 4, 2).reshape(T, W, CI, H)
    kt = weights.reshape(27 * CI, NH * HALF)
    dma = pltpu.SemaphoreType.DMA
    bf16, f32 = jnp.bfloat16, jnp.float32
    gin, gk = pl.pallas_call(
        functools.partial(kernel, rscale),
        out_shape=(jax.ShapeDtypeStruct((T, W, CI, H), bf16),
                   jax.ShapeDtypeStruct((27, CO, CI), f32)),
        in_specs=[pl.BlockSpec(memory_space=pltpu.MemorySpace.HBM)] * 3,
        out_specs=(pl.BlockSpec(memory_space=pltpu.VMEM),) * 2,
        scratch_shapes=[
            pltpu.VMEM((T, W, CI, H), bf16),
            pltpu.VMEM((T, W, CI, H), bf16),
            pltpu.VMEM((27 * CI, NH * HALF), bf16),
            pltpu.VMEM((NX, NZ, CI, POS), bf16),
            pltpu.VMEM((NX * NZ, 3 * CI, POS), bf16),
            pltpu.VMEM((NH, NY, 2, CI, POS), bf16),
            pltpu.VMEM((NZ, CI, POS), bf16),
            pltpu.VMEM((NX, NZ, CO, POS), bf16),
            pltpu.VMEM((27 * CI, POS), f32),
            pltpu.VMEM((CI, POS), f32),
            pltpu.VMEM((CI, POS), f32),
            pltpu.VMEM((CI, POS), f32),
            pltpu.VMEM((9 * CO, 3 * CI), f32),
            dma((3,)), dma, dma, dma((2, NY - 1)), dma((2, NY - 1)), dma((2,)), dma((2,)),
            dma((NZ - 1,)), dma((NZ - 1,)), dma((NZ, NX - 1)), dma((NZ, NX - 1)),
            dma((2,)), dma((NZ,)), dma((2,)), dma,
            dma((NY - 1,)), dma((NY - 1,)), dma((NY,)), dma((NY,)), dma((2,)), dma((2,)),
        ],
        compiler_params=pltpu.CompilerParams(
            collective_id=0, has_side_effects=True, vmem_limit_bytes=60 << 20),
    )(xt, gt, kt)
    grad_in = gin.reshape(1, T, W, CI, H).transpose(0, 1, 4, 2, 3)
    grad_kernel = gk.reshape(3, 3, 3, CO, CI).transpose(0, 1, 2, 4, 3)
    return grad_in, grad_kernel


def solution(mesh):
    return jax.shard_map(
        body,
        mesh=mesh,
        in_specs=(
            P(None, None, None, "lon", "ch"),
            P(None, None, None, "lon", "ch"),
            P(None, None, None, "ch", None),
        ),
        out_specs=(P(None, None, None, "lon", "ch"), P(None, None, None, "ch", "lon")),
        check_vma=False,
    )
```

time: 60.2 us -> 56.5 us (0.939)
  Pallas kernels: 55.1 us -> 52.5 us
  local copies, waits for them, and re-layouts: 4.16 us -> 3.11 us
    pallas_call x1, Pallas kernels: 55.1 us -> 52.5 us  [body(): pl.pallas_call(functools.partial(kernel, rscale), out_shape=(jax.ShapeDty...]
    unnamed x8 -> x2, local copies, waits for them, and re-layouts: 4.16 us -> 3.11 us
where the time goes in v2:
time: 56.5 us; the launch traced here: 56.3 us
  Pallas kernels  52.5 us (93%)
  local copies, waits for them, and re-layouts  3.11 us (6%)
  between operations  0.64 us (1%)
    pallas_call x1, Pallas kernels, body(): pl.pallas_call(functools.partial(kernel, rscale), out_shape=(jax.ShapeDty...  52.5 us
    unnamed x2, local copies, waits for them, and re-layouts  3.11 us

profile of v2, /device:TPU:1, one launch (start us, length us, event | category | flops | bytes accessed | tf_op | source)
XLA Modules:
  0.0 56.3 jit_solution(15955655476098193746)
XLA Ops:
  0.6 52.5 %shard_map.50 = (bf16[4,2,32,48]{3,2,1,0:T(8,128)(2,1)}, f32[27,16,32]{2,1,0:T(8,128)}) custom-call(bf16[4,2,32,48]{3,2,1,0:T(8,128)(2,1)} %bitcast.15, bf16[4,2,32,48]{3,2,1,0:T(8,128)(2,1)} %bitcast.16, bf16[864,512]{1,0:T(8,128)(2,1)} %bitcast.13), custom_call_target="tpu_custom_call" | custom-call | tf_op jit(solution)/shard_map/pallas_call | solution.py:306
  53.2 1.5 %copy.7 = bf16[1,4,48,2,32]{2,4,3,1,0:T(8,128)(2,1)} copy(bf16[1,4,48,2,32]{2,4,3,1,0:T(8,128)(2,1)} %bitcast.17) | data formatting | bytes 49152
  54.6 1.6 %copy.8 = f32[3,3,3,32,16]{3,4,2,1,0:T(8,128)} copy(f32[3,3,3,32,16]{3,4,2,1,0:T(8,128)} %bitcast.14) | data formatting | bytes 110592

commit v3 on v2

--- a/solution.py
+++ b/solution.py
@@ -113,9 +113,6 @@
         abuf[z] = gall[zh, y, core]
 
     gy = [go(remote(mine, mine, gy_s.at[0, d], gy_r.at[0, d], y_ids[d])) for d in range(NY - 1)]
-    own = xg.at[x, z]
-    xz = {d: go(remote(own, own, xz_s.at[d], xz_r.at[d], z_ids[d])) for d in NEAR}
-    xx = [go(remote(own, own, xx_s.at[0, e], xx_r.at[0, e], x_ids[e])) for e in range(NX - 1)]
 
     def pass_x(ds):
         for d in ds:
@@ -131,8 +128,9 @@
     for c in gy:
         c.wait_recv()
     sib0 = to_core(zh, 0)
-    pass_x(NEAR[:4])
-
+    own = xg.at[x, z]
+    xz = {d: go(remote(own, own, xz_s.at[d], xz_r.at[d], z_ids[d])) for d in NEAR}
+    xx = [go(remote(own, own, xx_s.at[0, e], xx_r.at[0, e], x_ids[e])) for e in range(NX - 1)]
     swap.wait_recv()
     other = gall.at[1 - zh, y, core]
     gy1 = [go(remote(other, other, gy_s.at[1, d], gy_r.at[1, d], y_ids[d])) for d in range(NY - 1)]
@@ -158,7 +156,7 @@
             def _():
                 gg[x] = abuf[:, CO * r:CO * (r + 1)]
 
-    pass_x(NEAR[4:])
+    pass_x(NEAR)
 
     lane = lax.broadcasted_iota(jnp.int32, (1, POS), 1)
     hh = lax.rem(lane, H)
@@ -172,6 +170,23 @@
     load_k.wait()
     sib0.wait_recv()
     prod[...] = half_product(zh)
+    def ay_copy(d):
+        slab = gg.at[y]
+        return remote(slab, slab, ay_s.at[d], ay_r.at[d], y_ids[d])
+
+    def ac_copy(d):
+        slab = gg.at[lax.rem(y + NY - d, NY)]
+        return remote(slab, slab, ac_s.at[d], ac_r.at[d], sib_id)
+
+    @pl.when(carries)
+    def _():
+        @pl.when(jnp.logical_not(b_self))
+        def _():
+            b_copy(0).wait_recv()
+        for d in range(NY - 1):
+            ay_copy(d).start()
+        ac_copy(0).start()
+
     for c in gy1:
         c.wait_recv()
     sib1 = to_core(1 - zh, 1)
@@ -200,25 +215,14 @@
     to_left = go(remote(zbuf, zr, ha_s.at[0], ha_r.at[0], left_id))
     to_right = go(remote(zbuf, zl, ha_s.at[1], ha_r.at[1], right_id))
 
-    def ay_copy(d):
-        slab = gg.at[y]
-        return remote(slab, slab, ay_s.at[d], ay_r.at[d], y_ids[d])
-
-    def ac_copy(d):
-        slab = gg.at[lax.rem(y + NY - d, NY)]
-        return remote(slab, slab, ac_s.at[d], ac_r.at[d], sib_id)
-
-    @pl.when(carries)
-    def _():
-        @pl.when(jnp.logical_not(b_self))
-        def _():
-            b_copy(0).wait_recv()
-        for d in range(NY - 1):
-            ay_copy(d).start()
-        ac_copy(0).start()
-
     mid = tap_sum(1)
     inner = jnp.where(low, sum2, sum0)
+    @pl.when(carries)
+    def _():
+        for d in range(NY - 1):
+            ay_copy(d).wait_recv()
+            ac_copy(d + 1).start()
+
     for c in xx:
         c.wait_recv()
     zero = jnp.zeros((), jnp.bfloat16)
@@ -229,21 +233,6 @@
         xs[i, 0:CI] = jnp.where(hh != 0, shift_lanes(xb, 1), zero)
         xs[i, CI:2 * CI] = xb
         xs[i, 2 * CI:] = jnp.where(hh != H - 1, shift_lanes(xb, -1), zero)
-
-    @pl.when(carries)
-    def _():
-        for d in range(NY - 1):
-            ay_copy(d).wait_recv()
-            ac_copy(d + 1).start()
-
-    to_left.wait_recv()
-    to_right.wait_recv()
-    grad = mid + shift_lanes(inner + jnp.where(low, zr[...], zl[...]), COL)
-    grad = grad.astype(jnp.bfloat16)
-    for w in range(W):
-        for t in range(T):
-            o = w * COL + t * H
-            gin_ref[t, w] = grad[:, o:o + H]
 
     @pl.when(jnp.logical_not(carries))
     def _():
@@ -273,6 +262,15 @@
             r = (a * 3 + e) * CO
             for c in range(3):
                 gk_ref[(a * 3 + c) * 3 + e] = acc[r:r + CO, c * CI:(c + 1) * CI] * rscale
+
+    to_left.wait_recv()
+    to_right.wait_recv()
+    grad = mid + shift_lanes(inner + jnp.where(low, zr[...], zl[...]), COL)
+    grad = grad.astype(jnp.bfloat16)
+    for w in range(W):
+        for t in range(T):
+            o = w * COL + t * H
+            gin_ref[t, w] = grad[:, o:o + H]
 
     for c in sends:
         c.wait_send()
@@ -329,8 +327,8 @@
             dma((NY - 1,)), dma((NY - 1,)), dma((NY,)), dma((NY,)), dma((2,)), dma((2,)),
         ],
         compiler_params=pltpu.CompilerParams(
-            collective_id=0, has_side_effects=True, vmem_limit_bytes=60 << 20),
-    )(xt, gt, kt)
+            collective_id=0, has_side_effects=True, vmem_limit_bytes=32 << 20),
+    )(*(pltpu.with_memory_space_constraint(v, pltpu.MemorySpace.HBM) for v in (xt, gt, kt)))
     grad_in = gin.reshape(1, T, W, CI, H).transpose(0, 1, 4, 2, 3)
     grad_kernel = gk.reshape(3, 3, 3, CO, CI).transpose(0, 1, 2, 4, 3)
     return grad_in, grad_kernel

time: 56.5 us -> 50.3 us (0.89)
  Pallas kernels: 52.5 us -> 47.7 us
  local copies, waits for them, and re-layouts: 3.11 us -> 1.32 us
    pallas_call x1, Pallas kernels: 52.5 us -> 47.7 us  [body(): pl.pallas_call(functools.partial(kernel, rscale), out_shape=(jax.ShapeDty...]
    unnamed x2, local copies, waits for them, and re-layouts: 3.11 us -> 1.32 us
where the time goes in v3:
time: 50.3 us; the launch traced here: 49.7 us
  Pallas kernels  47.7 us (95%)
  local copies, waits for them, and re-layouts  1.32 us (3%)
  between operations  0.64 us (1%)
    pallas_call x1, Pallas kernels, body(): pl.pallas_call(functools.partial(kernel, rscale), out_shape=(jax.ShapeDty...  47.7 us
    unnamed x2, local copies, waits for them, and re-layouts  1.32 us

profile of v3, /device:TPU:1, one launch (start us, length us, event | category | flops | bytes accessed | tf_op | source)
XLA Modules:
  0.0 49.7 jit_solution(7252481826244657027)
XLA Ops:
  0.6 47.7 %shard_map.50 = (bf16[4,2,32,48]{3,2,1,0:T(8,128)(2,1)S(1)}, f32[27,16,32]{2,1,0:T(8,128)S(1)}) custom-call(bf16[4,2,32,48]{3,2,1,0:T(8,128)(2,1)} %bitcast.16, bf16[4,2,32,48]{3,2,1,0:T(8,128)(2,1)} %bitcast.17, bf16[864,512]{1,0:T(8,128)(2,1)} %bitcast.15), custom_call_target="tpu_custom_call" | custom-call | tf_op jit(solution)/shard_map/pallas_call | solution.py:304
  48.3 0.6 %copy.7 = bf16[1,4,48,2,32]{2,4,3,1,0:T(8,128)(2,1)} copy(bf16[1,4,48,2,32]{2,4,3,1,0:T(8,128)(2,1)S(1)} %bitcast.14) | data formatting | bytes 49152
  49.0 0.7 %copy.8 = f32[3,3,3,32,16]{3,4,2,1,0:T(8,128)} copy(f32[3,3,3,32,16]{3,4,2,1,0:T(8,128)S(1)} %bitcast.13) | data formatting | bytes 110592

commit v4 on v3

--- a/solution.py
+++ b/solution.py
@@ -30,7 +30,7 @@
 
 
 def kernel(rscale, x_hbm, g_hbm, k_hbm, gin_ref, gk_ref,
-           x_ref, g_ref, k_ref, xg, xs, gall, abuf, gg, prod, zbuf, zl, zr, acc,
+           x_ref, g_ref, k_ref, xg, xs, gall, abuf, gg, gr, prod, zbuf, zl, zr, acc,
            load_s, swap_s, swap_r, gy_s, gy_r, core_s, core_r,
            xz_s, xz_r, xx_s, xx_r, a_s, a_r, b_s, b_r, ay_s, ay_r, ac_s, ac_r, ha_s, ha_r):
     lon, ch = lax.axis_index("lon"), lax.axis_index("ch")
@@ -162,6 +162,16 @@
     hh = lax.rem(lane, H)
     tt = lax.rem(lane // H, T)
     low = lane < COL
+    zero = jnp.zeros((), jnp.bfloat16)
+
+    def shift_x(sl):
+        @pl.loop(0, NZ)
+        def _(i):
+            xb = xg[sl, i]
+            xs[sl, i, 0:CI] = jnp.where(hh != 0, shift_lanes(xb, 1), zero)
+            xs[sl, i, CI:2 * CI] = xb
+            xs[sl, i, 2 * CI:] = jnp.where(hh != H - 1, shift_lanes(xb, -1), zero)
+
 
     def half_product(h):
         cols = pl.ds(pl.multiple_of(h * HALF, HALF), HALF)
@@ -217,22 +227,19 @@
 
     mid = tap_sum(1)
     inner = jnp.where(low, sum2, sum0)
+
+    shift_x(x)
+
     @pl.when(carries)
     def _():
         for d in range(NY - 1):
             ay_copy(d).wait_recv()
             ac_copy(d + 1).start()
 
-    for c in xx:
-        c.wait_recv()
-    zero = jnp.zeros((), jnp.bfloat16)
-
-    @pl.loop(0, NX * NZ)
-    def _(i):
-        xb = xg[i // NZ, lax.rem(i, NZ)]
-        xs[i, 0:CI] = jnp.where(hh != 0, shift_lanes(xb, 1), zero)
-        xs[i, CI:2 * CI] = xb
-        xs[i, 2 * CI:] = jnp.where(hh != H - 1, shift_lanes(xb, -1), zero)
+    for d in range(NX - 1):
+        for c in xx[d::NX - 1]:
+            c.wait_recv()
+        shift_x(lax.rem(x + NX - 1 - d, NX))
 
     @pl.when(jnp.logical_not(carries))
     def _():
@@ -244,18 +251,22 @@
     @pl.loop(0, NZ)
     def _(zz):
         for xn in range(NX):
-            here = gg[xn, zz]
-            after = gg[xn + 1, zz] if xn < NX - 1 else gg[0, lax.rem(zz + 1, NZ)]
-            before = gg[xn - 1, zz] if xn > 0 else gg[NX - 1, lax.rem(zz + NZ - 1, NZ)]
-            rh = shift_lanes(here, COL)
-            e0 = jnp.where(low, rh, shift_lanes(after, COL))
-            e2 = jnp.where(low, shift_lanes(before, COL), rh)
-            ge = jnp.concatenate([e0, here, e2], axis=0)
+            gr[xn, zz] = shift_lanes(gg[xn, zz], COL)
+
+    @pl.loop(0, NZ)
+    def _(zz):
+        cols = []
+        for xn in range(NX):
+            here = gr[xn, zz]
+            after = gr[xn + 1, zz] if xn < NX - 1 else gr[0, lax.rem(zz + 1, NZ)]
+            before = gr[xn - 1, zz] if xn > 0 else gr[NX - 1, lax.rem(zz + NZ - 1, NZ)]
+            ge = jnp.concatenate([jnp.where(low, here, after), gg[xn, zz], jnp.where(low, before, here)], axis=0)
             a0 = jnp.where(tt != T - 1, shift_lanes(ge, -H), zero)
             a2 = jnp.where(tt != 0, shift_lanes(ge, H), zero)
-            gs = jnp.concatenate([a0, ge, a2], axis=0)
-            acc[...] += lax.dot_general(
-                gs, xs[xn * NZ + zz], (((1,), (1,)), ((), ())), preferred_element_type=jnp.float32)
+            cols.append(jnp.concatenate([a0, ge, a2], axis=0))
+        acc[...] += lax.dot_general(
+            jnp.concatenate(cols, axis=1), jnp.concatenate([xs[xn, zz] for xn in range(NX)], axis=1),
+            (((1,), (1,)), ((), ())), preferred_element_type=jnp.float32)
 
     for a in range(3):
         for e in range(3):
@@ -312,9 +323,10 @@
             pltpu.VMEM((T, W, CI, H), bf16),
             pltpu.VMEM((27 * CI, NH * HALF), bf16),
             pltpu.VMEM((NX, NZ, CI, POS), bf16),
-            pltpu.VMEM((NX * NZ, 3 * CI, POS), bf16),
+            pltpu.VMEM((NX, NZ, 3 * CI, POS), bf16),
             pltpu.VMEM((NH, NY, 2, CI, POS), bf16),
             pltpu.VMEM((NZ, CI, POS), bf16),
+            pltpu.VMEM((NX, NZ, CO, POS), bf16),
             pltpu.VMEM((NX, NZ, CO, POS), bf16),
             pltpu.VMEM((27 * CI, POS), f32),
             pltpu.VMEM((CI, POS), f32),

time: 50.3 us -> 48.5 us (0.964)
  Pallas kernels: 47.7 us -> 46.4 us
    pallas_call x1, Pallas kernels: 47.7 us -> 46.4 us  [body(): pl.pallas_call(functools.partial(kernel, rscale), out_shape=(jax.ShapeDty...]
where the time goes in v4:
time: 48.5 us; the launch traced here: 48.4 us
  Pallas kernels  46.4 us (96%)
  local copies, waits for them, and re-layouts  1.32 us (3%)
  between operations  0.64 us (1%)
    pallas_call x1, Pallas kernels, body(): pl.pallas_call(functools.partial(kernel, rscale), out_shape=(jax.ShapeDty...  46.4 us
    unnamed x2, local copies, waits for them, and re-layouts  1.32 us

profile of v4, /device:TPU:1, one launch (start us, length us, event | category | flops | bytes accessed | tf_op | source)
XLA Modules:
  0.0 48.4 jit_solution(15299198363060872870)
XLA Ops:
  0.6 46.4 %shard_map.50 = (bf16[4,2,32,48]{3,2,1,0:T(8,128)(2,1)S(1)}, f32[27,16,32]{2,1,0:T(8,128)S(1)}) custom-call(bf16[4,2,32,48]{3,2,1,0:T(8,128)(2,1)} %bitcast.16, bf16[4,2,32,48]{3,2,1,0:T(8,128)(2,1)} %bitcast.17, bf16[864,512]{1,0:T(8,128)(2,1)} %bitcast.15), custom_call_target="tpu_custom_call" | custom-call | tf_op jit(solution)/shard_map/pallas_call | solution.py:315
  47.0 0.6 %copy.7 = bf16[1,4,48,2,32]{2,4,3,1,0:T(8,128)(2,1)} copy(bf16[1,4,48,2,32]{2,4,3,1,0:T(8,128)(2,1)S(1)} %bitcast.14) | data formatting | bytes 49152
  47.7 0.7 %copy.8 = f32[3,3,3,32,16]{3,4,2,1,0:T(8,128)} copy(f32[3,3,3,32,16]{3,4,2,1,0:T(8,128)S(1)} %bitcast.13) | data formatting | bytes 110592

commit v5 on v4

--- a/solution.py
+++ b/solution.py
@@ -97,7 +97,6 @@
         return copy
 
     mine = gall.at[zh, y, core]
-    swap = go(remote(mine, mine, swap_s, swap_r, swap_id))
     a_z = zh * NY + y
     go(remote(mine, abuf.at[z], a_s.at[0], a_r.at[z], at(z=a_z, zh=1 - zh)))
 
@@ -112,6 +111,7 @@
     def _():
         abuf[z] = gall[zh, y, core]
 
+    swap = go(remote(mine, mine, swap_s, swap_r, swap_id))
     gy = [go(remote(mine, mine, gy_s.at[0, d], gy_r.at[0, d], y_ids[d])) for d in range(NY - 1)]
 
     def pass_x(ds):
@@ -133,7 +133,7 @@
     xx = [go(remote(own, own, xx_s.at[0, e], xx_r.at[0, e], x_ids[e])) for e in range(NX - 1)]
     swap.wait_recv()
     other = gall.at[1 - zh, y, core]
-    gy1 = [go(remote(other, other, gy_s.at[1, d], gy_r.at[1, d], y_ids[d])) for d in range(NY - 1)]
+    gy1 = [go(remote(other, other, gy_s.at[1, d], gy_r.at[1, d], y_ids[d])) for d in (1, 0, 2)]
 
     def b_copy(r):
         return remote(abuf.at[:, pl.ds(CO * r, CO)], gg.at[x], b_s.at[r], b_r, at(x=core * 2 + r, y=x))
@@ -164,13 +164,11 @@
     low = lane < COL
     zero = jnp.zeros((), jnp.bfloat16)
 
-    def shift_x(sl):
-        @pl.loop(0, NZ)
-        def _(i):
-            xb = xg[sl, i]
-            xs[sl, i, 0:CI] = jnp.where(hh != 0, shift_lanes(xb, 1), zero)
-            xs[sl, i, CI:2 * CI] = xb
-            xs[sl, i, 2 * CI:] = jnp.where(hh != H - 1, shift_lanes(xb, -1), zero)
+    def shift_x(sl, i):
+        xb = xg[sl, i]
+        xs[sl, i, 0:CI] = jnp.where(hh != 0, shift_lanes(xb, 1), zero)
+        xs[sl, i, CI:2 * CI] = xb
+        xs[sl, i, 2 * CI:] = jnp.where(hh != H - 1, shift_lanes(xb, -1), zero)
 
 
     def half_product(h):
@@ -193,7 +191,7 @@
         @pl.when(jnp.logical_not(b_self))
         def _():
             b_copy(0).wait_recv()
-        for d in range(NY - 1):
+        for d in (1, 0, 2):
             ay_copy(d).start()
         ac_copy(0).start()
 
@@ -228,7 +226,9 @@
     mid = tap_sum(1)
     inner = jnp.where(low, sum2, sum0)
 
-    shift_x(x)
+    @pl.loop(0, NZ)
+    def _(i):
+        shift_x(x, i)
 
     @pl.when(carries)
     def _():
@@ -236,10 +236,13 @@
             ay_copy(d).wait_recv()
             ac_copy(d + 1).start()
 
-    for d in range(NX - 1):
-        for c in xx[d::NX - 1]:
+    for k, d in enumerate((NZ - 1,) + NEAR):
+        for c in xx[k * (NX - 1):(k + 1) * (NX - 1)]:
             c.wait_recv()
-        shift_x(lax.rem(x + NX - 1 - d, NX))
+
+        @pl.loop(1, NX)
+        def _(e):
+            shift_x(lax.rem(x + NX - e, NX), lax.rem(z + 2 * NZ - 1 - d, NZ))
 
     @pl.when(jnp.logical_not(carries))
     def _():

time: 48.5 us -> 48.4 us (level)
  no operation moved by 1% of the time
where the time goes in v5:
time: 48.4 us; the launch traced here: 48.3 us
  Pallas kernels  46.3 us (96%)
  local copies, waits for them, and re-layouts  1.32 us (3%)
  between operations  0.64 us (1%)
    pallas_call x1, Pallas kernels, body(): pl.pallas_call(functools.partial(kernel, rscale), out_shape=(jax.ShapeDty...  46.3 us
    unnamed x2, local copies, waits for them, and re-layouts  1.32 us

profile of v5, /device:TPU:1, one launch (start us, length us, event | category | flops | bytes accessed | tf_op | source)
XLA Modules:
  0.0 48.3 jit_solution(7678019779799890907)
XLA Ops:
  0.6 46.3 %shard_map.50 = (bf16[4,2,32,48]{3,2,1,0:T(8,128)(2,1)S(1)}, f32[27,16,32]{2,1,0:T(8,128)S(1)}) custom-call(bf16[4,2,32,48]{3,2,1,0:T(8,128)(2,1)} %bitcast.16, bf16[4,2,32,48]{3,2,1,0:T(8,128)(2,1)} %bitcast.17, bf16[864,512]{1,0:T(8,128)(2,1)} %bitcast.15), custom_call_target="tpu_custom_call" | custom-call | tf_op jit(solution)/shard_map/pallas_call | solution.py:318
  47.0 0.6 %copy.7 = bf16[1,4,48,2,32]{2,4,3,1,0:T(8,128)(2,1)} copy(bf16[1,4,48,2,32]{2,4,3,1,0:T(8,128)(2,1)S(1)} %bitcast.14) | data formatting | bytes 49152
  47.6 0.7 %copy.8 = f32[3,3,3,32,16]{3,4,2,1,0:T(8,128)} copy(f32[3,3,3,32,16]{3,4,2,1,0:T(8,128)S(1)} %bitcast.13) | data formatting | bytes 110592

commit v6 on v5

--- a/solution.py
+++ b/solution.py
@@ -85,8 +85,6 @@
 
     load_g.wait()
     gall[zh, y, core] = pack(g_ref)
-    load_x.wait()
-    xg[x, z] = pack(x_ref)
     pl.semaphore_wait(barrier, len(partners) + 1 + jnp.where(turn, 2 - (carries & (x == y)).astype(jnp.int32), 0))
 
     sends = []
@@ -125,6 +123,8 @@
         part = gall.at[h, :, core]
         return go(remote(part, part, core_s.at[i], core_r.at[i], sib_id))
 
+    load_x.wait()
+    xg[x, z] = pack(x_ref)
     for c in gy:
         c.wait_recv()
     sib0 = to_core(zh, 0)

time: 48.4 us -> 48.4 us (level)
  no operation moved by 1% of the time
where the time goes in v6:
time: 48.4 us; the launch traced here: 48.3 us
  Pallas kernels  46.3 us (96%)
  local copies, waits for them, and re-layouts  1.32 us (3%)
  between operations  0.64 us (1%)
    pallas_call x1, Pallas kernels, body(): pl.pallas_call(functools.partial(kernel, rscale), out_shape=(jax.ShapeDty...  46.3 us
    unnamed x2, local copies, waits for them, and re-layouts  1.32 us

profile of v6, /device:TPU:1, one launch (start us, length us, event | category | flops | bytes accessed | tf_op | source)
XLA Modules:
  0.0 48.3 jit_solution(13273622584784553071)
XLA Ops:
  0.6 46.3 %shard_map.50 = (bf16[4,2,32,48]{3,2,1,0:T(8,128)(2,1)S(1)}, f32[27,16,32]{2,1,0:T(8,128)S(1)}) custom-call(bf16[4,2,32,48]{3,2,1,0:T(8,128)(2,1)} %bitcast.16, bf16[4,2,32,48]{3,2,1,0:T(8,128)(2,1)} %bitcast.17, bf16[864,512]{1,0:T(8,128)(2,1)} %bitcast.15), custom_call_target="tpu_custom_call" | custom-call | tf_op jit(solution)/shard_map/pallas_call | solution.py:318
  47.0 0.6 %copy.7 = bf16[1,4,48,2,32]{2,4,3,1,0:T(8,128)(2,1)} copy(bf16[1,4,48,2,32]{2,4,3,1,0:T(8,128)(2,1)S(1)} %bitcast.14) | data formatting | bytes 49152
  47.6 0.7 %copy.8 = f32[3,3,3,32,16]{3,4,2,1,0:T(8,128)} copy(f32[3,3,3,32,16]{3,4,2,1,0:T(8,128)S(1)} %bitcast.13) | data formatting | bytes 110592

commit v7 on v4

--- a/solution.py
+++ b/solution.py
@@ -85,8 +85,6 @@
 
     load_g.wait()
     gall[zh, y, core] = pack(g_ref)
-    load_x.wait()
-    xg[x, z] = pack(x_ref)
     pl.semaphore_wait(barrier, len(partners) + 1 + jnp.where(turn, 2 - (carries & (x == y)).astype(jnp.int32), 0))
 
     sends = []
@@ -97,7 +95,6 @@
         return copy
 
     mine = gall.at[zh, y, core]
-    swap = go(remote(mine, mine, swap_s, swap_r, swap_id))
     a_z = zh * NY + y
     go(remote(mine, abuf.at[z], a_s.at[0], a_r.at[z], at(z=a_z, zh=1 - zh)))
 
@@ -112,6 +109,7 @@
     def _():
         abuf[z] = gall[zh, y, core]
 
+    swap = go(remote(mine, mine, swap_s, swap_r, swap_id))
     gy = [go(remote(mine, mine, gy_s.at[0, d], gy_r.at[0, d], y_ids[d])) for d in range(NY - 1)]
 
     def pass_x(ds):
@@ -125,6 +123,8 @@
         part = gall.at[h, :, core]
         return go(remote(part, part, core_s.at[i], core_r.at[i], sib_id))
 
+    load_x.wait()
+    xg[x, z] = pack(x_ref)
     for c in gy:
         c.wait_recv()
     sib0 = to_core(zh, 0)

time: 48.5 us -> 48.5 us (level)
  no operation moved by 1% of the time
where the time goes in v7:
time: 48.5 us; the launch traced here: 48.4 us
  Pallas kernels  46.4 us (96%)
  local copies, waits for them, and re-layouts  1.32 us (3%)
  between operations  0.64 us (1%)
    pallas_call x1, Pallas kernels, body(): pl.pallas_call(functools.partial(kernel, rscale), out_shape=(jax.ShapeDty...  46.4 us
    unnamed x2, local copies, waits for them, and re-layouts  1.32 us

profile of v7, /device:TPU:1, one launch (start us, length us, event | category | flops | bytes accessed | tf_op | source)
XLA Modules:
  0.0 48.4 jit_solution(5092338064754863354)
XLA Ops:
  0.6 46.4 %shard_map.50 = (bf16[4,2,32,48]{3,2,1,0:T(8,128)(2,1)S(1)}, f32[27,16,32]{2,1,0:T(8,128)S(1)}) custom-call(bf16[4,2,32,48]{3,2,1,0:T(8,128)(2,1)} %bitcast.16, bf16[4,2,32,48]{3,2,1,0:T(8,128)(2,1)} %bitcast.17, bf16[864,512]{1,0:T(8,128)(2,1)} %bitcast.15), custom_call_target="tpu_custom_call" | custom-call | tf_op jit(solution)/shard_map/pallas_call | solution.py:315
  47.0 0.6 %copy.7 = bf16[1,4,48,2,32]{2,4,3,1,0:T(8,128)(2,1)} copy(bf16[1,4,48,2,32]{2,4,3,1,0:T(8,128)(2,1)S(1)} %bitcast.14) | data formatting | bytes 49152
  47.7 0.7 %copy.8 = f32[3,3,3,32,16]{3,4,2,1,0:T(8,128)} copy(f32[3,3,3,32,16]{3,4,2,1,0:T(8,128)S(1)} %bitcast.13) | data formatting | bytes 110592
